TPU v7x, 32 devices: a whole 2x2x4 slice. The times are simulated.
32 devices in a mesh: cuts: 1, state: 32 (over z, y, x, core).
Axes of the slice: x: 2, y: 2, z: 4, core: 2. Of those that a mesh axis runs over, the one named last changes fastest.
Arguments:
- initial_states: bfloat16 [256, 32, 48, 128], P(('cuts', 'state')), may hold values from -36 to 36
- potential: float32 [32, 48, 128], replicated, may hold values from -1 to 0
- bounds: int32 [2], P('cuts'), may hold values from -32 to 159, as said below
Outputs:
- orthonormal: float32 [256, 196608], P('cuts', 'state')
Inputs may be any that keep to these rules, and one draw needn't show every extreme that they name: `bounds`: the first entry lies in -32 to -17, inside the spectrum of H, and the second in 136 to 159, above it; the anchor -1.125 lies below the spectrum.
All inputs are finite; a program needn't handle non-finite values.
Results may differ from a plain program's by a relative error of at most 0.0003.
Values sent between devices are 32-bit elements; how exact they have to be, the bound alone decides.
No kernel may reach another device: no remote copies, remote signals or barrier semaphores. Data moves between devices by JAX's collectives and lax.ppermute only.
A program may use at most 192 MiB of HBM per device.

v0:
```python
import math
import jax
import jax.numpy as jnp
from jax import lax
from jax.sharding import PartitionSpec as P

DEGREE = 16
STENCIL_NEAR = 4.0 / 3.0
STENCIL_FAR = -1.0 / 12.0
STENCIL_SELF = -5.0 / 2.0
ANCHOR_VALUE = -1.125


def laplace_periodic(values, axis_dim):
    near_sum = jnp.roll(values, 1, axis_dim) + jnp.roll(values, -1, axis_dim)
    far_sum = jnp.roll(values, 2, axis_dim) + jnp.roll(values, -2, axis_dim)
    return STENCIL_NEAR * near_sum + STENCIL_FAR * far_sum


def laplace_walled(values):
    extent = values.shape[1]
    padded = jnp.pad(values, ((0, 0), (2, 2), (0, 0), (0, 0)))
    near_sum = padded[:, 1 : extent + 1] + padded[:, 3 : extent + 3]
    far_sum = padded[:, 0:extent] + padded[:, 4 : extent + 4]
    return STENCIL_NEAR * near_sum + STENCIL_FAR * far_sum


def apply_hamiltonian(values, potential):
    laplace = 3.0 * STENCIL_SELF * values + laplace_walled(values)
    laplace = laplace + laplace_periodic(values, 2) + laplace_periodic(values, 3)
    return -0.5 * laplace + potential[None] * values


def filter_states(states, potential, bounds):
    low_end = bounds[0].astype(jnp.float32) / 64.0
    high_end = bounds[1].astype(jnp.float32) / 16.0
    half_width = (high_end - low_end) / 2.0
    centre = (high_end + low_end) / 2.0
    sigma_now = half_width / (ANCHOR_VALUE - centre)
    tau_value = 2.0 / sigma_now
    current = (apply_hamiltonian(states, potential) - centre * states) * (sigma_now / half_width)

    def degree_step(degree, carried):
        previous, current, sigma_now = carried
        sigma_next = 1.0 / (tau_value - sigma_now)
        latest = (apply_hamiltonian(current, potential) - centre * current) * (
            2.0 * sigma_next / half_width
        )
        latest = latest - sigma_now * sigma_next * previous
        return (current, latest, sigma_next)

    carried = lax.fori_loop(1, DEGREE, degree_step, (states, current, sigma_now))
    return carried[1]


def outer_product(left, right):
    return lax.dot_general(
        left,
        right,
        (((1,), (1,)), ((), ())),
        precision=lax.Precision.HIGHEST,
        preferred_element_type=jnp.float32,
    )


def per_device(initial_states, potential, bounds):
    filtered = filter_states(initial_states.astype(jnp.float32), potential, bounds)
    points = filtered.shape[1] * filtered.shape[2] * filtered.shape[3]
    flat = filtered.reshape(filtered.shape[0], points)
    row_block = lax.all_to_all(flat, "state", split_axis=1, concat_axis=0, tiled=True)
    gram_local = outer_product(row_block, row_block)
    gram_total = lax.psum(gram_local, "state")
    factor = jnp.linalg.cholesky(gram_total)
    solved = lax.linalg.triangular_solve(factor, row_block, left_side=True, lower=True)
    return solved * math.sqrt(points)


def solution(mesh):
    return jax.shard_map(
        per_device,
        mesh=mesh,
        in_specs=(P(("cuts", "state"), None, None, None), P(), P("cuts")),
        out_specs=P("cuts", "state"),
        check_vma=False,
    )
```

profile of v0, /device:TPU:0, one launch (start us, length us, event | category | flops | bytes accessed | tf_op | source)
XLA Modules:
  0.0 1869.4 jit_solution(1136967705735163389)
XLA Ops:
  9.2 8.4 fusion.55
  50.8 37.2 %fusion.28 = f32[8,32,48,128]{3,2,1,0:T(8,128)} fusion(f32[8,32,48,128]{3,2,1,0:T(8,128)} %convert_element_type.16, f32[8,32,47,128]{3,2,1,0:T(8,128)} %get-tuple-element.170, f32[8,32,1,128]{3,2,1,0:T(1,128)S(1)} %get-tuple-element.172, f32[8,32,1,128]{3,2,1,0:T(1,128)S(1)} %get-tuple-element.171, f32[8,32,47,128]{3,2,1,0:T(8,128)} %get-tuple-element.169, ...), kind=kLoop, calls=%fused_computation.43 | loop fusion | flops 51904512 | bytes 63701000 | tf_op jit(solution)/shard_map/mul | solution.py:41
  87.9 1411.8 %while.17 = (s32[]{:T(128)}, f32[8,32,48,128]{3,2,1,0:T(8,128)}, f32[8,32,48,128]{3,2,1,0:T(8,128)}, f32[]{:T(128)}, f32[32,48,128]{2,1,0:T(8,128)S(1)}, /*index...) while((s32[]{:T(128)}, f32[8,32,48,128]{3,2,1,0:T(8,128)}, ...), condition=%wide.region_1.2_spmd, body=%wide.region_0.1_spmd.sunk | while | flops 55050248 | bytes 243007824 | solution.py:52
  88.0 10.6 fusion.78
  104.3 6.7 fusion.82
  132.7 39.8 %fusion.86 = f32[8,32,48,128]{3,2,1,0:T(8,128)} fusion(f32[8,32,48,128]{3,2,1,0:T(8,128)} %get-tuple-element.306, f32[8,32,47,128]{3,2,1,0:T(8,128)} %get-tuple-element.271, f32[8,32,1,128]{3,2,1,0:T(1,128)} %get-tuple-element.272, f32[8,32,1,128]{3,2,1,0:T(1,128)S(1)} %get-tuple-element.273, f32[8,32,47,128]{3,2,1,0:T(8,128)} %get-tuple-element.274, ...), kind=kLoop, calls=%fused_computation.14.clone.1 | loop fusion | flops 55050240 | bytes 69992464 | tf_op jit(solution)/shard_map/while/body/eval_jaxpr/sub | solution.py:49
  181.4 10.6 fusion.78
  197.7 6.7 fusion.82
  226.1 39.8 %fusion.86 = f32[8,32,48,128]{3,2,1,0:T(8,128)} fusion(f32[8,32,48,128]{3,2,1,0:T(8,128)} %get-tuple-element.306, f32[8,32,47,128]{3,2,1,0:T(8,128)} %get-tuple-element.271, f32[8,32,1,128]{3,2,1,0:T(1,128)} %get-tuple-element.272, f32[8,32,1,128]{3,2,1,0:T(1,128)S(1)} %get-tuple-element.273, f32[8,32,47,128]{3,2,1,0:T(8,128)} %get-tuple-element.274, ...), kind=kLoop, calls=%fused_computation.14.clone.1 | loop fusion | flops 55050240 | bytes 69992464 | tf_op jit(solution)/shard_map/while/body/eval_jaxpr/sub | solution.py:49
  274.7 10.6 fusion.78
  291.1 6.7 fusion.82
  319.5 39.8 %fusion.86 = f32[8,32,48,128]{3,2,1,0:T(8,128)} fusion(f32[8,32,48,128]{3,2,1,0:T(8,128)} %get-tuple-element.306, f32[8,32,47,128]{3,2,1,0:T(8,128)} %get-tuple-element.271, f32[8,32,1,128]{3,2,1,0:T(1,128)} %get-tuple-element.272, f32[8,32,1,128]{3,2,1,0:T(1,128)S(1)} %get-tuple-element.273, f32[8,32,47,128]{3,2,1,0:T(8,128)} %get-tuple-element.274, ...), kind=kLoop, calls=%fused_computation.14.clone.1 | loop fusion | flops 55050240 | bytes 69992464 | tf_op jit(solution)/shard_map/while/body/eval_jaxpr/sub | solution.py:49
  368.1 10.6 fusion.78
  412.8 39.8 %fusion.86 = f32[8,32,48,128]{3,2,1,0:T(8,128)} fusion(f32[8,32,48,128]{3,2,1,0:T(8,128)} %get-tuple-element.306, f32[8,32,47,128]{3,2,1,0:T(8,128)} %get-tuple-element.271, f32[8,32,1,128]{3,2,1,0:T(1,128)} %get-tuple-element.272, f32[8,32,1,128]{3,2,1,0:T(1,128)S(1)} %get-tuple-element.273, f32[8,32,47,128]{3,2,1,0:T(8,128)} %get-tuple-element.274, ...), kind=kLoop, calls=%fused_computation.14.clone.1 | loop fusion | flops 55050240 | bytes 69992464 | tf_op jit(solution)/shard_map/while/body/eval_jaxpr/sub | solution.py:49
  461.5 10.6 fusion.78
  477.8 6.7 fusion.82
  506.2 39.8 %fusion.86 = f32[8,32,48,128]{3,2,1,0:T(8,128)} fusion(f32[8,32,48,128]{3,2,1,0:T(8,128)} %get-tuple-element.306, f32[8,32,47,128]{3,2,1,0:T(8,128)} %get-tuple-element.271, f32[8,32,1,128]{3,2,1,0:T(1,128)} %get-tuple-element.272, f32[8,32,1,128]{3,2,1,0:T(1,128)S(1)} %get-tuple-element.273, f32[8,32,47,128]{3,2,1,0:T(8,128)} %get-tuple-element.274, ...), kind=kLoop, calls=%fused_computation.14.clone.1 | loop fusion | flops 55050240 | bytes 69992464 | tf_op jit(solution)/shard_map/while/body/eval_jaxpr/sub | solution.py:49
  554.9 10.6 fusion.78
  599.6 39.8 %fusion.86 = f32[8,32,48,128]{3,2,1,0:T(8,128)} fusion(f32[8,32,48,128]{3,2,1,0:T(8,128)} %get-tuple-element.306, f32[8,32,47,128]{3,2,1,0:T(8,128)} %get-tuple-element.271, f32[8,32,1,128]{3,2,1,0:T(1,128)} %get-tuple-element.272, f32[8,32,1,128]{3,2,1,0:T(1,128)S(1)} %get-tuple-element.273, f32[8,32,47,128]{3,2,1,0:T(8,128)} %get-tuple-element.274, ...), kind=kLoop, calls=%fused_computation.14.clone.1 | loop fusion | flops 55050240 | bytes 69992464 | tf_op jit(solution)/shard_map/while/body/eval_jaxpr/sub | solution.py:49
  648.3 10.6 fusion.78
  664.6 6.7 fusion.82
  693.0 39.8 %fusion.86 = f32[8,32,48,128]{3,2,1,0:T(8,128)} fusion(f32[8,32,48,128]{3,2,1,0:T(8,128)} %get-tuple-element.306, f32[8,32,47,128]{3,2,1,0:T(8,128)} %get-tuple-element.271, f32[8,32,1,128]{3,2,1,0:T(1,128)} %get-tuple-element.272, f32[8,32,1,128]{3,2,1,0:T(1,128)S(1)} %get-tuple-element.273, f32[8,32,47,128]{3,2,1,0:T(8,128)} %get-tuple-element.274, ...), kind=kLoop, calls=%fused_computation.14.clone.1 | loop fusion | flops 55050240 | bytes 69992464 | tf_op jit(solution)/shard_map/while/body/eval_jaxpr/sub | solution.py:49
  741.7 10.6 fusion.78
  758.0 6.7 fusion.82
  786.4 39.8 %fusion.86 = f32[8,32,48,128]{3,2,1,0:T(8,128)} fusion(f32[8,32,48,128]{3,2,1,0:T(8,128)} %get-tuple-element.306, f32[8,32,47,128]{3,2,1,0:T(8,128)} %get-tuple-element.271, f32[8,32,1,128]{3,2,1,0:T(1,128)} %get-tuple-element.272, f32[8,32,1,128]{3,2,1,0:T(1,128)S(1)} %get-tuple-element.273, f32[8,32,47,128]{3,2,1,0:T(8,128)} %get-tuple-element.274, ...), kind=kLoop, calls=%fused_computation.14.clone.1 | loop fusion | flops 55050240 | bytes 69992464 | tf_op jit(solution)/shard_map/while/body/eval_jaxpr/sub | solution.py:49
  835.0 10.6 fusion.78
  851.4 6.7 fusion.82
  879.8 39.8 %fusion.86 = f32[8,32,48,128]{3,2,1,0:T(8,128)} fusion(f32[8,32,48,128]{3,2,1,0:T(8,128)} %get-tuple-element.306, f32[8,32,47,128]{3,2,1,0:T(8,128)} %get-tuple-element.271, f32[8,32,1,128]{3,2,1,0:T(1,128)} %get-tuple-element.272, f32[8,32,1,128]{3,2,1,0:T(1,128)S(1)} %get-tuple-element.273, f32[8,32,47,128]{3,2,1,0:T(8,128)} %get-tuple-element.274, ...), kind=kLoop, calls=%fused_computation.14.clone.1 | loop fusion | flops 55050240 | bytes 69992464 | tf_op jit(solution)/shard_map/while/body/eval_jaxpr/sub | solution.py:49
  928.4 10.6 fusion.78
  944.7 6.7 fusion.82
  973.1 39.8 %fusion.86 = f32[8,32,48,128]{3,2,1,0:T(8,128)} fusion(f32[8,32,48,128]{3,2,1,0:T(8,128)} %get-tuple-element.306, f32[8,32,47,128]{3,2,1,0:T(8,128)} %get-tuple-element.271, f32[8,32,1,128]{3,2,1,0:T(1,128)} %get-tuple-element.272, f32[8,32,1,128]{3,2,1,0:T(1,128)S(1)} %get-tuple-element.273, f32[8,32,47,128]{3,2,1,0:T(8,128)} %get-tuple-element.274, ...), kind=kLoop, calls=%fused_computation.14.clone.1 | loop fusion | flops 55050240 | bytes 69992464 | tf_op jit(solution)/shard_map/while/body/eval_jaxpr/sub | solution.py:49
  1021.8 10.6 fusion.78
  1066.5 39.8 %fusion.86 = f32[8,32,48,128]{3,2,1,0:T(8,128)} fusion(f32[8,32,48,128]{3,2,1,0:T(8,128)} %get-tuple-element.306, f32[8,32,47,128]{3,2,1,0:T(8,128)} %get-tuple-element.271, f32[8,32,1,128]{3,2,1,0:T(1,128)} %get-tuple-element.272, f32[8,32,1,128]{3,2,1,0:T(1,128)S(1)} %get-tuple-element.273, f32[8,32,47,128]{3,2,1,0:T(8,128)} %get-tuple-element.274, ...), kind=kLoop, calls=%fused_computation.14.clone.1 | loop fusion | flops 55050240 | bytes 69992464 | tf_op jit(solution)/shard_map/while/body/eval_jaxpr/sub | solution.py:49
  1115.2 10.6 fusion.78
  1131.5 6.7 fusion.82
  1159.9 39.8 %fusion.86 = f32[8,32,48,128]{3,2,1,0:T(8,128)} fusion(f32[8,32,48,128]{3,2,1,0:T(8,128)} %get-tuple-element.306, f32[8,32,47,128]{3,2,1,0:T(8,128)} %get-tuple-element.271, f32[8,32,1,128]{3,2,1,0:T(1,128)} %get-tuple-element.272, f32[8,32,1,128]{3,2,1,0:T(1,128)S(1)} %get-tuple-element.273, f32[8,32,47,128]{3,2,1,0:T(8,128)} %get-tuple-element.274, ...), kind=kLoop, calls=%fused_computation.14.clone.1 | loop fusion | flops 55050240 | bytes 69992464 | tf_op jit(solution)/shard_map/while/body/eval_jaxpr/sub | solution.py:49
  1208.6 10.6 fusion.78
  1253.3 39.8 %fusion.86 = f32[8,32,48,128]{3,2,1,0:T(8,128)} fusion(f32[8,32,48,128]{3,2,1,0:T(8,128)} %get-tuple-element.306, f32[8,32,47,128]{3,2,1,0:T(8,128)} %get-tuple-element.271, f32[8,32,1,128]{3,2,1,0:T(1,128)} %get-tuple-element.272, f32[8,32,1,128]{3,2,1,0:T(1,128)S(1)} %get-tuple-element.273, f32[8,32,47,128]{3,2,1,0:T(8,128)} %get-tuple-element.274, ...), kind=kLoop, calls=%fused_computation.14.clone.1 | loop fusion | flops 55050240 | bytes 69992464 | tf_op jit(solution)/shard_map/while/body/eval_jaxpr/sub | solution.py:49
  1302.0 10.6 fusion.78
  1346.7 39.8 %fusion.86 = f32[8,32,48,128]{3,2,1,0:T(8,128)} fusion(f32[8,32,48,128]{3,2,1,0:T(8,128)} %get-tuple-element.306, f32[8,32,47,128]{3,2,1,0:T(8,128)} %get-tuple-element.271, f32[8,32,1,128]{3,2,1,0:T(1,128)} %get-tuple-element.272, f32[8,32,1,128]{3,2,1,0:T(1,128)S(1)} %get-tuple-element.273, f32[8,32,47,128]{3,2,1,0:T(8,128)} %get-tuple-element.274, ...), kind=kLoop, calls=%fused_computation.14.clone.1 | loop fusion | flops 55050240 | bytes 69992464 | tf_op jit(solution)/shard_map/while/body/eval_jaxpr/sub | solution.py:49
  1395.3 10.6 fusion.78
  1440.1 39.8 %fusion.86 = f32[8,32,48,128]{3,2,1,0:T(8,128)} fusion(f32[8,32,48,128]{3,2,1,0:T(8,128)} %get-tuple-element.306, f32[8,32,47,128]{3,2,1,0:T(8,128)} %get-tuple-element.271, f32[8,32,1,128]{3,2,1,0:T(1,128)} %get-tuple-element.272, f32[8,32,1,128]{3,2,1,0:T(1,128)S(1)} %get-tuple-element.273, f32[8,32,47,128]{3,2,1,0:T(8,128)} %get-tuple-element.274, ...), kind=kLoop, calls=%fused_computation.14.clone.1 | loop fusion | flops 55050240 | bytes 69992464 | tf_op jit(solution)/shard_map/while/body/eval_jaxpr/sub | solution.py:49
  1506.2 145.7 %all_to_all.19 = f32[8,32,6144]{2,0,1:T(8,128)S(1)} all-to-all(f32[8,32,6144]{2,0,1:T(8,128)S(1)} %bitcast.52), channel_id=1, replica_groups=mesh['cuts'=1,'state'=32] {'state'}, dimensions={1} | all-to-all | bytes 12582912 | tf_op jit(solution)/shard_map/all_to_all | solution.py:70
  1660.5 125.8 %all-reduce.5.cloned.1.call-done = f32[256,256]{0,1:T(8,128)} async-done(((f32[256,256]{0,1:T(8,128)}), f32[256,256]{0,1:T(8,128)}) %all-reduce.5.cloned.1.call-update) | async-done | bytes 262160 | tf_op jit(solution)/shard_map/psum | solution.py:72
  1788.4 11.7 cholesky.50
  1800.2 9.8 custom-call.14
  1810.5 11.9 cholesky.105
  1828.5 19.7 %custom-call.15 = f32[2,128,128]{1,2,0:T(8,128)S(1)} custom-call(f32[2,128,128]{2,1,0:T(8,128)S(1)} %get-tuple-element.114), custom_call_target="InvertDiagBlocksLowerTriangular" | custom-call | tf_op jit(solution)/shard_map/triangular_solve | solution.py:74
  (306 shorter events, 657.7 us)
Async XLA Ops:
  6.5 1779.8 %all-reduce.5.cloned.1.call-start = ((), (), s32[]{:S(2)}) async-start(), calls=%async_computation.1 | async-start | bytes 524288 | tf_op jit(solution)/shard_map/psum | solution.py:72
  9.2 8.4 copy-start
  88.0 10.6 slice-start
  88.0 10.6 slice-start.1
  172.5 6.1 copy-start.1
  181.4 10.6 slice-start
  181.4 10.6 slice-start.1
  265.8 6.1 copy-start.1
  274.7 10.6 slice-start
  274.7 10.6 slice-start.1
  359.2 6.1 copy-start.1
  368.1 10.6 slice-start
  368.1 10.6 slice-start.1
  452.6 6.1 copy-start.1
  461.5 10.6 slice-start
  461.5 10.6 slice-start.1
  546.0 6.1 copy-start.1
  554.9 10.6 slice-start
  554.9 10.6 slice-start.1
  639.4 6.1 copy-start.1
  648.3 10.6 slice-start
  648.3 10.6 slice-start.1
  732.8 6.1 copy-start.1
  741.7 10.6 slice-start
  741.7 10.6 slice-start.1
  826.1 6.1 copy-start.1
  835.0 10.6 slice-start
  835.0 10.6 slice-start.1
  919.5 6.1 copy-start.1
  928.4 10.6 slice-start
  928.4 10.6 slice-start.1
  1012.9 6.1 copy-start.1
  1021.8 10.6 slice-start
  1021.8 10.6 slice-start.1
  1106.3 6.1 copy-start.1
  1115.2 10.6 slice-start
  1115.2 10.6 slice-start.1
  1199.7 6.1 copy-start.1
  1208.6 10.6 slice-start
  1208.6 10.6 slice-start.1
  1293.1 6.1 copy-start.1
  1301.9 10.6 slice-start
  1301.9 10.6 slice-start.1
  1386.4 6.1 copy-start.1
  1395.3 10.6 slice-start
  1395.3 10.6 slice-start.1
  1479.8 6.1 copy-start.1
  1848.2 4.9 copy-start.3
  (17 other events, 48.2 us)
Sparse Core Ops, SparseCore 0:
  1660.6 125.6 all-reduce.4
where the time goes:
time: 1880 us; the launch traced here: 1870 us
  local copies, waits for them, and re-layouts  856 us (46%)
  other arithmetic  695 us (37%)
  blocking collectives  146 us (8%)
  waiting for transfers between devices  126 us (7%)
    sub x15, other arithmetic, degree_step(): latest = latest - sigma_now * sigma_next * previous  596 us
    slice x64, local copies, waits for them, and re-layouts, laplace_periodic(): near_sum = jnp.roll(values, 1, axis_dim) + jnp.roll(values, -1, axis_dim)  390 us
    slice x64, local copies, waits for them, and re-layouts, laplace_periodic(): far_sum = jnp.roll(values, 2, axis_dim) + jnp.roll(values, -2, axis_dim)  317 us
    all_to_all x1, blocking collectives, per_device(): lax.all_to_all(flat, 'state', split_axis=1, concat_axis=0, tiled=True)  146 us
    while x150, local copies, waits for them, and re-layouts  133 us
    psum x1, waiting for transfers between devices, per_device(): gram_total = lax.psum(gram_local, 'state')  126 us
  transfers between devices with their start and end apart: 1, of which 1 were waited for; matrix products, arithmetic and copies ran while one was open for 0% of the time, Pallas kernels for 0%

commit v1 on v0

--- a/solution.py
+++ b/solution.py
@@ -67,7 +67,10 @@
     filtered = filter_states(initial_states.astype(jnp.float32), potential, bounds)
     points = filtered.shape[1] * filtered.shape[2] * filtered.shape[3]
     flat = filtered.reshape(filtered.shape[0], points)
-    row_block = lax.all_to_all(flat, "state", split_axis=1, concat_axis=0, tiled=True)
+    size = lax.axis_size("state")
+    blocks = jnp.stack(jnp.split(flat, size, axis=1), axis=0)
+    blocks = lax.all_to_all(blocks, "state", split_axis=0, concat_axis=0)
+    row_block = jnp.concatenate(blocks, axis=0)
     gram_local = outer_product(row_block, row_block)
     gram_total = lax.psum(gram_local, "state")
     factor = jnp.linalg.cholesky(gram_total)

time: 1880 us -> 1880 us (level)
    while x151 -> x150, local copies, waits for them, and re-layouts: 140 us -> 133 us
where the time goes in v1:
time: 1880 us; the launch traced here: 1870 us
  local copies, waits for them, and re-layouts  860 us (46%)
  other arithmetic  695 us (37%)
  blocking collectives  146 us (8%)
  waiting for transfers between devices  126 us (7%)
    sub x15, other arithmetic, degree_step(): latest = latest - sigma_now * sigma_next * previous  596 us
    slice x64, local copies, waits for them, and re-layouts, laplace_periodic(): near_sum = jnp.roll(values, 1, axis_dim) + jnp.roll(values, -1, axis_dim)  390 us
    slice x64, local copies, waits for them, and re-layouts, laplace_periodic(): far_sum = jnp.roll(values, 2, axis_dim) + jnp.roll(values, -2, axis_dim)  317 us
    all_to_all x1, blocking collectives, per_device(): blocks = lax.all_to_all(blocks, 'state', split_axis=0, concat_axis=0)  146 us
    while x150, local copies, waits for them, and re-layouts  133 us
    psum x1, waiting for transfers between devices, per_device(): gram_total = lax.psum(gram_local, 'state')  126 us
  transfers between devices with their start and end apart: 1, of which 1 were waited for; matrix products, arithmetic and copies ran while one was open for 0% of the time, Pallas kernels for 0%

profile of v1, /device:TPU:0, one launch (start us, length us, event | category | flops | bytes accessed | tf_op | source)
XLA Modules:
  0.0 1873.3 jit_solution(16462598495090936513)
XLA Ops:
  9.2 8.4 fusion.87
  50.8 37.2 %fusion.28 = f32[8,32,48,128]{3,2,1,0:T(8,128)} fusion(f32[8,32,48,128]{3,2,1,0:T(8,128)} %convert_element_type.16, f32[8,32,47,128]{3,2,1,0:T(8,128)} %get-tuple-element.170, f32[8,32,1,128]{3,2,1,0:T(1,128)S(1)} %get-tuple-element.172, f32[8,32,1,128]{3,2,1,0:T(1,128)S(1)} %get-tuple-element.171, f32[8,32,47,128]{3,2,1,0:T(8,128)} %get-tuple-element.169, ...), kind=kLoop, calls=%fused_computation.43 | loop fusion | flops 51904512 | bytes 63701000 | tf_op jit(solution)/shard_map/mul | solution.py:41
  87.9 1412.2 %while.17 = (s32[]{:T(128)}, f32[8,32,48,128]{3,2,1,0:T(8,128)}, f32[8,32,48,128]{3,2,1,0:T(8,128)}, f32[]{:T(128)}, f32[32,48,128]{2,1,0:T(8,128)S(1)}, /*index...) while((s32[]{:T(128)}, f32[8,32,48,128]{3,2,1,0:T(8,128)}, ...), condition=%wide.region_1.2_spmd, body=%wide.region_0.1_spmd.sunk | while | flops 55050248 | bytes 243007824 | solution.py:52
  88.0 10.6 fusion.110
  104.3 6.7 fusion.114
  132.7 39.8 %fusion.118 = f32[8,32,48,128]{3,2,1,0:T(8,128)} fusion(f32[8,32,48,128]{3,2,1,0:T(8,128)} %get-tuple-element.306, f32[8,32,47,128]{3,2,1,0:T(8,128)} %get-tuple-element.271, f32[8,32,1,128]{3,2,1,0:T(1,128)} %get-tuple-element.272, f32[8,32,1,128]{3,2,1,0:T(1,128)S(1)} %get-tuple-element.273, f32[8,32,47,128]{3,2,1,0:T(8,128)} %get-tuple-element.274, ...), kind=kLoop, calls=%fused_computation.14.clone.1 | loop fusion | flops 55050240 | bytes 69992464 | tf_op jit(solution)/shard_map/while/body/eval_jaxpr/sub | solution.py:49
  181.4 10.6 fusion.110
  197.7 6.7 fusion.114
  226.1 39.8 %fusion.118 = f32[8,32,48,128]{3,2,1,0:T(8,128)} fusion(f32[8,32,48,128]{3,2,1,0:T(8,128)} %get-tuple-element.306, f32[8,32,47,128]{3,2,1,0:T(8,128)} %get-tuple-element.271, f32[8,32,1,128]{3,2,1,0:T(1,128)} %get-tuple-element.272, f32[8,32,1,128]{3,2,1,0:T(1,128)S(1)} %get-tuple-element.273, f32[8,32,47,128]{3,2,1,0:T(8,128)} %get-tuple-element.274, ...), kind=kLoop, calls=%fused_computation.14.clone.1 | loop fusion | flops 55050240 | bytes 69992464 | tf_op jit(solution)/shard_map/while/body/eval_jaxpr/sub | solution.py:49
  274.7 10.6 fusion.110
  291.1 6.7 fusion.114
  319.5 39.8 %fusion.118 = f32[8,32,48,128]{3,2,1,0:T(8,128)} fusion(f32[8,32,48,128]{3,2,1,0:T(8,128)} %get-tuple-element.306, f32[8,32,47,128]{3,2,1,0:T(8,128)} %get-tuple-element.271, f32[8,32,1,128]{3,2,1,0:T(1,128)} %get-tuple-element.272, f32[8,32,1,128]{3,2,1,0:T(1,128)S(1)} %get-tuple-element.273, f32[8,32,47,128]{3,2,1,0:T(8,128)} %get-tuple-element.274, ...), kind=kLoop, calls=%fused_computation.14.clone.1 | loop fusion | flops 55050240 | bytes 69992464 | tf_op jit(solution)/shard_map/while/body/eval_jaxpr/sub | solution.py:49
  368.1 10.6 fusion.110
  412.8 39.8 %fusion.118 = f32[8,32,48,128]{3,2,1,0:T(8,128)} fusion(f32[8,32,48,128]{3,2,1,0:T(8,128)} %get-tuple-element.306, f32[8,32,47,128]{3,2,1,0:T(8,128)} %get-tuple-element.271, f32[8,32,1,128]{3,2,1,0:T(1,128)} %get-tuple-element.272, f32[8,32,1,128]{3,2,1,0:T(1,128)S(1)} %get-tuple-element.273, f32[8,32,47,128]{3,2,1,0:T(8,128)} %get-tuple-element.274, ...), kind=kLoop, calls=%fused_computation.14.clone.1 | loop fusion | flops 55050240 | bytes 69992464 | tf_op jit(solution)/shard_map/while/body/eval_jaxpr/sub | solution.py:49
  461.5 10.6 fusion.110
  477.8 6.7 fusion.114
  506.2 39.8 %fusion.118 = f32[8,32,48,128]{3,2,1,0:T(8,128)} fusion(f32[8,32,48,128]{3,2,1,0:T(8,128)} %get-tuple-element.306, f32[8,32,47,128]{3,2,1,0:T(8,128)} %get-tuple-element.271, f32[8,32,1,128]{3,2,1,0:T(1,128)} %get-tuple-element.272, f32[8,32,1,128]{3,2,1,0:T(1,128)S(1)} %get-tuple-element.273, f32[8,32,47,128]{3,2,1,0:T(8,128)} %get-tuple-element.274, ...), kind=kLoop, calls=%fused_computation.14.clone.1 | loop fusion | flops 55050240 | bytes 69992464 | tf_op jit(solution)/shard_map/while/body/eval_jaxpr/sub | solution.py:49
  554.9 10.6 fusion.110
  599.6 39.8 %fusion.118 = f32[8,32,48,128]{3,2,1,0:T(8,128)} fusion(f32[8,32,48,128]{3,2,1,0:T(8,128)} %get-tuple-element.306, f32[8,32,47,128]{3,2,1,0:T(8,128)} %get-tuple-element.271, f32[8,32,1,128]{3,2,1,0:T(1,128)} %get-tuple-element.272, f32[8,32,1,128]{3,2,1,0:T(1,128)S(1)} %get-tuple-element.273, f32[8,32,47,128]{3,2,1,0:T(8,128)} %get-tuple-element.274, ...), kind=kLoop, calls=%fused_computation.14.clone.1 | loop fusion | flops 55050240 | bytes 69992464 | tf_op jit(solution)/shard_map/while/body/eval_jaxpr/sub | solution.py:49
  648.3 10.6 fusion.110
  664.6 6.7 fusion.114
  693.0 39.8 %fusion.118 = f32[8,32,48,128]{3,2,1,0:T(8,128)} fusion(f32[8,32,48,128]{3,2,1,0:T(8,128)} %get-tuple-element.306, f32[8,32,47,128]{3,2,1,0:T(8,128)} %get-tuple-element.271, f32[8,32,1,128]{3,2,1,0:T(1,128)} %get-tuple-element.272, f32[8,32,1,128]{3,2,1,0:T(1,128)S(1)} %get-tuple-element.273, f32[8,32,47,128]{3,2,1,0:T(8,128)} %get-tuple-element.274, ...), kind=kLoop, calls=%fused_computation.14.clone.1 | loop fusion | flops 55050240 | bytes 69992464 | tf_op jit(solution)/shard_map/while/body/eval_jaxpr/sub | solution.py:49
  741.7 10.6 fusion.110
  758.0 6.7 fusion.114
  786.4 39.8 %fusion.118 = f32[8,32,48,128]{3,2,1,0:T(8,128)} fusion(f32[8,32,48,128]{3,2,1,0:T(8,128)} %get-tuple-element.306, f32[8,32,47,128]{3,2,1,0:T(8,128)} %get-tuple-element.271, f32[8,32,1,128]{3,2,1,0:T(1,128)} %get-tuple-element.272, f32[8,32,1,128]{3,2,1,0:T(1,128)S(1)} %get-tuple-element.273, f32[8,32,47,128]{3,2,1,0:T(8,128)} %get-tuple-element.274, ...), kind=kLoop, calls=%fused_computation.14.clone.1 | loop fusion | flops 55050240 | bytes 69992464 | tf_op jit(solution)/shard_map/while/body/eval_jaxpr/sub | solution.py:49
  835.0 10.6 fusion.110
  851.4 6.7 fusion.114
  879.8 39.8 %fusion.118 = f32[8,32,48,128]{3,2,1,0:T(8,128)} fusion(f32[8,32,48,128]{3,2,1,0:T(8,128)} %get-tuple-element.306, f32[8,32,47,128]{3,2,1,0:T(8,128)} %get-tuple-element.271, f32[8,32,1,128]{3,2,1,0:T(1,128)} %get-tuple-element.272, f32[8,32,1,128]{3,2,1,0:T(1,128)S(1)} %get-tuple-element.273, f32[8,32,47,128]{3,2,1,0:T(8,128)} %get-tuple-element.274, ...), kind=kLoop, calls=%fused_computation.14.clone.1 | loop fusion | flops 55050240 | bytes 69992464 | tf_op jit(solution)/shard_map/while/body/eval_jaxpr/sub | solution.py:49
  928.4 10.6 fusion.110
  944.7 6.7 fusion.114
  973.1 39.8 %fusion.118 = f32[8,32,48,128]{3,2,1,0:T(8,128)} fusion(f32[8,32,48,128]{3,2,1,0:T(8,128)} %get-tuple-element.306, f32[8,32,47,128]{3,2,1,0:T(8,128)} %get-tuple-element.271, f32[8,32,1,128]{3,2,1,0:T(1,128)} %get-tuple-element.272, f32[8,32,1,128]{3,2,1,0:T(1,128)S(1)} %get-tuple-element.273, f32[8,32,47,128]{3,2,1,0:T(8,128)} %get-tuple-element.274, ...), kind=kLoop, calls=%fused_computation.14.clone.1 | loop fusion | flops 55050240 | bytes 69992464 | tf_op jit(solution)/shard_map/while/body/eval_jaxpr/sub | solution.py:49
  1021.8 10.6 fusion.110
  1066.5 39.8 %fusion.118 = f32[8,32,48,128]{3,2,1,0:T(8,128)} fusion(f32[8,32,48,128]{3,2,1,0:T(8,128)} %get-tuple-element.306, f32[8,32,47,128]{3,2,1,0:T(8,128)} %get-tuple-element.271, f32[8,32,1,128]{3,2,1,0:T(1,128)} %get-tuple-element.272, f32[8,32,1,128]{3,2,1,0:T(1,128)S(1)} %get-tuple-element.273, f32[8,32,47,128]{3,2,1,0:T(8,128)} %get-tuple-element.274, ...), kind=kLoop, calls=%fused_computation.14.clone.1 | loop fusion | flops 55050240 | bytes 69992464 | tf_op jit(solution)/shard_map/while/body/eval_jaxpr/sub | solution.py:49
  1115.2 10.6 fusion.110
  1159.9 39.8 %fusion.118 = f32[8,32,48,128]{3,2,1,0:T(8,128)} fusion(f32[8,32,48,128]{3,2,1,0:T(8,128)} %get-tuple-element.306, f32[8,32,47,128]{3,2,1,0:T(8,128)} %get-tuple-element.271, f32[8,32,1,128]{3,2,1,0:T(1,128)} %get-tuple-element.272, f32[8,32,1,128]{3,2,1,0:T(1,128)S(1)} %get-tuple-element.273, f32[8,32,47,128]{3,2,1,0:T(8,128)} %get-tuple-element.274, ...), kind=kLoop, calls=%fused_computation.14.clone.1 | loop fusion | flops 55050240 | bytes 69992464 | tf_op jit(solution)/shard_map/while/body/eval_jaxpr/sub | solution.py:49
  1208.6 10.6 fusion.110
  1253.3 39.8 %fusion.118 = f32[8,32,48,128]{3,2,1,0:T(8,128)} fusion(f32[8,32,48,128]{3,2,1,0:T(8,128)} %get-tuple-element.306, f32[8,32,47,128]{3,2,1,0:T(8,128)} %get-tuple-element.271, f32[8,32,1,128]{3,2,1,0:T(1,128)} %get-tuple-element.272, f32[8,32,1,128]{3,2,1,0:T(1,128)S(1)} %get-tuple-element.273, f32[8,32,47,128]{3,2,1,0:T(8,128)} %get-tuple-element.274, ...), kind=kLoop, calls=%fused_computation.14.clone.1 | loop fusion | flops 55050240 | bytes 69992464 | tf_op jit(solution)/shard_map/while/body/eval_jaxpr/sub | solution.py:49
  1302.0 10.6 fusion.110
  1346.7 39.8 %fusion.118 = f32[8,32,48,128]{3,2,1,0:T(8,128)} fusion(f32[8,32,48,128]{3,2,1,0:T(8,128)} %get-tuple-element.306, f32[8,32,47,128]{3,2,1,0:T(8,128)} %get-tuple-element.271, f32[8,32,1,128]{3,2,1,0:T(1,128)} %get-tuple-element.272, f32[8,32,1,128]{3,2,1,0:T(1,128)S(1)} %get-tuple-element.273, f32[8,32,47,128]{3,2,1,0:T(8,128)} %get-tuple-element.274, ...), kind=kLoop, calls=%fused_computation.14.clone.1 | loop fusion | flops 55050240 | bytes 69992464 | tf_op jit(solution)/shard_map/while/body/eval_jaxpr/sub | solution.py:49
  1395.3 10.6 fusion.110
  1440.1 39.8 %fusion.118 = f32[8,32,48,128]{3,2,1,0:T(8,128)} fusion(f32[8,32,48,128]{3,2,1,0:T(8,128)} %get-tuple-element.306, f32[8,32,47,128]{3,2,1,0:T(8,128)} %get-tuple-element.271, f32[8,32,1,128]{3,2,1,0:T(1,128)} %get-tuple-element.272, f32[8,32,1,128]{3,2,1,0:T(1,128)S(1)} %get-tuple-element.273, f32[8,32,47,128]{3,2,1,0:T(8,128)} %get-tuple-element.274, ...), kind=kLoop, calls=%fused_computation.14.clone.1 | loop fusion | flops 55050240 | bytes 69992464 | tf_op jit(solution)/shard_map/while/body/eval_jaxpr/sub | solution.py:49
  1500.2 9.2 copy.9
  1510.2 145.7 %all_to_all.5 = f32[32,8,6144]{2,1,0:T(8,128)S(1)} all-to-all(f32[32,8,6144]{2,1,0:T(8,128)S(1)} %fusion.41), channel_id=1, replica_groups=mesh['cuts'=1,'state'=32] {'state'}, dimensions={0} | all-to-all | bytes 12582912 | tf_op jit(solution)/shard_map/all_to_all | solution.py:72
  1664.5 125.8 %all-reduce.5.cloned.1.call-done = f32[256,256]{0,1:T(8,128)} async-done(((f32[256,256]{0,1:T(8,128)}), f32[256,256]{0,1:T(8,128)}) %all-reduce.5.cloned.1.call-update) | async-done | bytes 262160 | tf_op jit(solution)/shard_map/psum | solution.py:75
  1792.4 11.7 cholesky.50
  1804.2 9.8 custom-call.14
  1814.5 11.9 cholesky.105
  1832.5 19.7 %custom-call.15 = f32[2,128,128]{1,2,0:T(8,128)S(1)} custom-call(f32[2,128,128]{2,1,0:T(8,128)S(1)} %get-tuple-element.114), custom_call_target="InvertDiagBlocksLowerTriangular" | custom-call | tf_op jit(solution)/shard_map/triangular_solve | solution.py:77
  (338 shorter events, 658.5 us)
Async XLA Ops:
  6.5 1783.8 %all-reduce.5.cloned.1.call-start = ((), (), s32[]{:S(2)}) async-start(), calls=%async_computation.1 | async-start | bytes 524288 | tf_op jit(solution)/shard_map/psum | solution.py:75
  9.2 8.4 copy-start
  88.0 10.6 slice-start
  88.0 10.6 slice-start.1
  172.5 6.1 copy-start.1
  181.4 10.6 slice-start
  181.4 10.6 slice-start.1
  265.8 6.1 copy-start.1
  274.7 10.6 slice-start
  274.7 10.6 slice-start.1
  359.2 6.1 copy-start.1
  368.1 10.6 slice-start
  368.1 10.6 slice-start.1
  452.6 6.1 copy-start.1
  461.5 10.6 slice-start
  461.5 10.6 slice-start.1
  546.0 6.1 copy-start.1
  554.9 10.6 slice-start
  554.9 10.6 slice-start.1
  639.4 6.1 copy-start.1
  648.3 10.6 slice-start
  648.3 10.6 slice-start.1
  732.8 6.1 copy-start.1
  741.7 10.6 slice-start
  741.7 10.6 slice-start.1
  826.1 6.1 copy-start.1
  835.0 10.6 slice-start
  835.0 10.6 slice-start.1
  919.5 6.1 copy-start.1
  928.4 10.6 slice-start
  928.4 10.6 slice-start.1
  1012.9 6.1 copy-start.1
  1021.8 10.6 slice-start
  1021.8 10.6 slice-start.1
  1106.3 6.1 copy-start.1
  1115.2 10.6 slice-start
  1115.2 10.6 slice-start.1
  1199.7 6.1 copy-start.1
  1208.6 10.6 slice-start
  1208.6 10.6 slice-start.1
  1293.1 6.1 copy-start.1
  1301.9 10.6 slice-start
  1301.9 10.6 slice-start.1
  1386.4 6.1 copy-start.1
  1395.3 10.6 slice-start
  1395.3 10.6 slice-start.1
  1479.8 6.1 copy-start.1
  1852.2 4.9 copy-start.3
  (17 other events, 48.2 us)
Sparse Core Ops, SparseCore 0:
  1664.6 125.6 all-reduce.4
